TPU v7x, 32 devices: a whole 2x2x4 slice. The times are simulated.
32 devices in a mesh: row: 8 (over z, y), col: 4 (over x, core).
Axes of the slice: x: 2, y: 2, z: 4, core: 2. Of those that a mesh axis runs over, the one named last changes fastest.
Arguments:
- ancestor_inverse: float32 [12288, 12288], P('row', 'col'), may hold values from -5 to 320, as said below
- panel_one: float32 [12288, 256], P(('row', 'col')), may hold values from -0.015625 to 0.015625
- struct_one: int32 [10752], replicated, may hold values from 0 to 12287, as said below
- lower_one: float32 [256, 256], replicated, may hold values from -1 to 2, as said below
- panel_two: float32 [12288, 256], P(('row', 'col')), may hold values from -0.015625 to 0.015625
- struct_two: int32 [9216], replicated, may hold values from 0 to 12287, as said below
- panel_above: float32 [256, 256], replicated, may hold values from -0.375 to 0.375
- lower_two: float32 [256, 256], replicated, may hold values from -1 to 2, as said below
- tile_owner: int32 [192, 1], P(('col', 'row')), may hold values from 0 to 3; in each aligned block of 6 rows (0 to 5, 6 to 11, ...) at most 2 rows name the same one
Outputs:
- inverse_one: float32 [12288, 256], P(('col', 'row'))
- diag_one: float32 [256, 256], replicated
- cross_two: float32 [256, 256], replicated
- diag_two: float32 [256, 256], replicated
- delivered: float32 [256, 64, 256], P(('row', 'col'))
Inputs may be any that keep to these rules, and one draw needn't show every extreme that they name: ancestor_inverse is exactly symmetric and positive definite. `struct_one`: 10752 distinct row numbers of the ancestor block. `struct_two`: 9216 distinct entries of struct_one. `lower_one`: lower triangular with a positive diagonal. `lower_two`: lower triangular with a positive diagonal. `tile_owner`: within each aligned block of 6 entries (the tiles of one device) no value appears more than 2 times; in some block a value appears exactly 2 times.
All inputs are finite; a program needn't handle non-finite values.
Results may differ from a plain program's by a relative error of at most 0.00007.
Values sent between devices are 32-bit elements; how exact they have to be, the bound alone decides.
A program may use at most 64 MiB of HBM per device.

v0:
```python
import jax
import jax.numpy as jnp
from jax import lax
from jax.sharding import PartitionSpec as P

ANC = 12288
CAP = 2


def matmul(left, right):
    return jnp.dot(left, right, precision=lax.Precision.HIGHEST, preferred_element_type=jnp.float32)


def contract_rows(left, right):
    return lax.dot_general(
        left,
        right,
        (((0,), (0,)), ((), ())),
        precision=lax.Precision.HIGHEST,
        preferred_element_type=jnp.float32,
    )


def product_term(ancestor_inverse, block_panel, placed_rows):
    return jnp.concatenate([contract_rows(ancestor_inverse, block_panel), placed_rows], axis=1)


def deliver(values, tile_owner, col_count):
    tile_count = tile_owner.shape[0]
    tile_rows = values.shape[0] // tile_count
    all_tiles = values.reshape(tile_count, tile_rows, values.shape[1])
    owner_col = tile_owner[:, 0]
    col_ids = jnp.arange(col_count, dtype=jnp.int32)
    onehot = (owner_col[:, None] == col_ids[None, :]).astype(jnp.int32)
    tile_rank = jnp.sum((jnp.cumsum(onehot, axis=0) - onehot) * onehot, axis=1)
    slot_index = jnp.arange(CAP, dtype=jnp.int32)
    select = (
        (owner_col[None, None, :] == col_ids[:, None, None])
        & (tile_rank[None, None, :] == slot_index[None, :, None])
    ).astype(jnp.float32)
    outgoing = jnp.einsum("cks,srb->ckrb", select, all_tiles, precision=lax.Precision.HIGHEST)
    incoming = lax.all_to_all(outgoing, "col", split_axis=0, concat_axis=0, tiled=True)
    return incoming.reshape(col_count * CAP, tile_rows, values.shape[1])


def local(
    ancestor_inverse,
    panel_one,
    struct_one,
    lower_one,
    panel_two,
    struct_two,
    panel_above,
    lower_two,
    tile_owner,
):
    row_count = lax.axis_size("row")
    col_count = lax.axis_size("col")
    row_index = lax.axis_index("row")
    col_index = lax.axis_index("col")
    block_ratio = row_count // col_count
    local_rows = panel_one.shape[0]
    inner_rows = ancestor_inverse.shape[0]
    column_rows = ancestor_inverse.shape[1]
    width = panel_one.shape[1]
    mask_one = jnp.zeros((ANC,), jnp.float32).at[struct_one].set(1.0)
    mask_two = jnp.zeros((ANC,), jnp.float32).at[struct_two].set(1.0)
    panel_start = (row_index * col_count + col_index) * local_rows
    result_start = (col_index * row_count + row_index) * local_rows
    local_one = panel_one * lax.dynamic_slice_in_dim(mask_one, panel_start, local_rows)[:, None]
    local_two = panel_two * lax.dynamic_slice_in_dim(mask_two, panel_start, local_rows)[:, None]
    result_mask_one = lax.dynamic_slice_in_dim(mask_one, result_start, local_rows)[:, None]
    result_mask_two = lax.dynamic_slice_in_dim(mask_two, result_start, local_rows)[:, None]
    owns_block = (row_index // block_ratio == col_index).astype(jnp.float32)
    block_offset = row_index % block_ratio * inner_rows

    def place(gathered):
        empty_rows = jnp.zeros((column_rows, gathered.shape[1]), jnp.float32)
        return lax.dynamic_update_slice_in_dim(empty_rows, gathered * owns_block, block_offset, 0)

    gathered_one = lax.all_gather(local_one, "col", axis=0, tiled=True)
    summed_one = lax.psum_scatter(
        product_term(ancestor_inverse, gathered_one, place(gathered_one)),
        "row",
        scatter_dimension=0,
        tiled=True,
    )
    gathered_two = lax.all_gather(local_two, "col", axis=0, tiled=True)
    summed_two = lax.psum_scatter(
        product_term(ancestor_inverse, gathered_two, place(gathered_two)),
        "row",
        scatter_dimension=0,
        tiled=True,
    )
    product_one = summed_one[:, :width]
    resident_one = summed_one[:, width:]
    product_two = summed_two[:, :width]
    resident_two = summed_two[:, width:]
    inverse_one = -product_one * result_mask_one
    partial_gram = contract_rows(resident_one, inverse_one)
    partial_cross = contract_rows(inverse_one, resident_two)
    gram_one, cross_sum = lax.psum((partial_gram, partial_cross), ("row", "col"))
    diag_one = matmul(lower_one.T, lower_one) - gram_one
    cross_two = -(cross_sum + matmul(diag_one, panel_above))
    inverse_two = -(product_two + matmul(inverse_one, panel_above)) * result_mask_two
    partial_second = contract_rows(resident_two, inverse_two)
    gram_two = lax.psum(partial_second, ("row", "col"))
    diag_two = matmul(lower_two.T, lower_two) - gram_two - matmul(panel_above.T, cross_two)
    delivered = deliver(inverse_two, tile_owner, col_count)
    return (inverse_one, diag_one, cross_two, diag_two, delivered)


def solution(mesh):
    return jax.shard_map(
        local,
        mesh=mesh,
        in_specs=(
            P("row", "col"),
            P(("row", "col"), None),
            P(),
            P(),
            P(("row", "col"), None),
            P(),
            P(),
            P(),
            P(("col", "row"), None),
        ),
        out_specs=(P(("col", "row"), None), P(), P(), P(), P(("row", "col"), None, None)),
        check_vma=False,
    )
```

profile of v0, /device:TPU:0, one launch (start us, length us, event | category | flops | bytes accessed | tf_op | source)
XLA Modules:
  0.0 510.6 jit_solution(6775725624319687121)
XLA Ops:
  7.2 0.8 compare_select_fusion
  8.1 1.2 copy.36
  9.2 39.8 %scatter_custom_fusion = f32[12288]{0:T(1024)S(1)} fusion(s32[10752]{0:T(1024)S(1)} %compare_select_fusion, f32[10752]{0:T(1024)S(1)} %broadcast.48, f32[]{:T(128)} %constant.23.clone.1), kind=kCustom, calls=%fused_computation.34 | custom fusion | bytes 49156 | tf_op jit(solution)/shard_map/scatter | solution.py:66
  49.2 0.8 broadcast_multiply_fusion.1
  50.0 1.2 copy.37
  51.2 0.8 compare_select_fusion.1
  52.0 34.2 %scatter_custom_fusion.1 = f32[12288]{0:T(1024)S(1)} fusion(s32[9216]{0:T(1024)S(1)} %compare_select_fusion.1, f32[9216]{0:T(1024)S(1)} %broadcast.49, f32[]{:T(128)} %constant.23.clone.1), kind=kCustom, calls=%fused_computation.32 | custom fusion | bytes 49156 | tf_op jit(solution)/shard_map/scatter | solution.py:67
  86.3 0.8 broadcast_multiply_fusion
  87.5 1.0 copy-done.1
  88.7 19.2 %convolution_bitcast_fusion.1 = f32[3072,256]{0,1:T(8,128)S(1)} fusion(f32[1536,256]{0,1:T(8,128)S(1)} %copy-done.1, f32[1536,3072]{1,0:T(8,128)} %param.9), kind=kOutput, calls=%fused_computation.5 | convolution fusion | flops 14495514624 | bytes 23592960 | tf_op jit(solution)/shard_map/dot_general | solution.py:15
  107.9 3.1 pad_maximum_fusion
  111.6 1.0 copy-done.2
  112.8 19.2 %convolution_bitcast_fusion = f32[3072,256]{0,1:T(8,128)S(1)} fusion(f32[1536,256]{0,1:T(8,128)S(1)} %copy-done.2, f32[1536,3072]{1,0:T(8,128)} %param.9), kind=kOutput, calls=%fused_computation.4 | convolution fusion | flops 14495514624 | bytes 23592960 | tf_op jit(solution)/shard_map/dot_general | solution.py:15
  132.0 3.0 pad_maximum_fusion.1
  136.0 96.0 %reduce-scatter.3.cloned.1.call-done = f32[384,512]{0,1:T(8,128)} async-done(((f32[3072,512]{0,1:T(8,128)}), f32[384,512]{0,1:T(8,128)}) %reduce-scatter.3.cloned.1.call-update) | async-done | bytes 786448 | tf_op jit(solution)/shard_map/reduce_scatter | solution.py:82
  232.0 1.0 fusion.9
  233.0 119.7 %reduce-scatter.5.cloned.1.call-done = f32[384,512]{0,1:T(8,128)} async-done(((f32[3072,512]{0,1:T(8,128)}), f32[384,512]{0,1:T(8,128)}) %reduce-scatter.5.cloned.1.call-update) | async-done | bytes 786448 | tf_op jit(solution)/shard_map/reduce_scatter | solution.py:89
  352.7 1.7 fusion.1
  354.6 0.7 fusion.4
  355.2 0.9 copy.42
  356.1 3.6 all-to-all-start
  359.8 1.3 fusion.10
  361.1 1.3 fusion.12
  362.5 1.3 fusion.7
  363.8 0.9 copy.43
  364.7 3.8 all-to-all-done
  368.5 128.8 %all-reduce.3.cloned.1.call-done = (f32[256,256]{1,0:T(8,128)}, f32[256,256]{1,0:T(8,128)}, f32[256,256]{1,0:T(8,128)}) async-done(((f32[256,256]{1,0:T(8,128)}, f32[256,256]{1,0:T(8,128)}, f32[256,256]{1,0:T(8,128)}), (f32[256,256]{1,0:T(8,128)}, f32[256,256]{1,0:T(8,128)}, f32[256,256]{1,0:T(8,128)})) %all-reduce.3.cloned.1.call-update) | async-done | bytes 786448 | tf_op jit(solution)/shard_map/psum | solution.py:102
  497.3 1.5 convolution_subtract_fusion.1
  498.8 1.4 fusion.3
  500.3 1.6 convolution_subtract_fusion
  502.0 1.3 fusion.2
  503.3 0.8 copy.59
  (44 shorter events, 2.7 us)
Async XLA Ops:
  7.2 345.5 %copy-start = (f32[256,256]{1,0:T(8,128)S(1)}, f32[256,256]{1,0:T(8,128)}, u32[]{:S(2)}) copy-start(f32[256,256]{1,0:T(8,128)} %param.15) | copy-start | bytes 786436
  7.2 80.0 %all-gather.3.cloned.1.call-start = ((), (), s32[]{:S(2)}) async-start(), calls=%async_computation.3 | async-start | bytes 1966080 | tf_op jit(solution)/shard_map/all_gather | solution.py:81
  50.0 61.3 %all-gather.5.cloned.1.call-start = ((), (), s32[]{:S(2)}) async-start(), calls=%async_computation.5 | async-start | bytes 1966080 | tf_op jit(solution)/shard_map/all_gather | solution.py:88
  87.1 144.9 %reduce-scatter.3.cloned.1.call-start = ((), (), s32[]{:S(2)}) async-start(), calls=%async_computation.4 | async-start | bytes 7077888 | tf_op jit(solution)/shard_map/reduce_scatter | solution.py:82
  87.2 1.4 copy-start.1
  111.0 241.7 %reduce-scatter.5.cloned.1.call-start = ((), (), s32[]{:S(2)}) async-start(), calls=%async_computation.6 | async-start | bytes 7077888 | tf_op jit(solution)/shard_map/reduce_scatter | solution.py:89
  111.3 1.4 copy-start.2
  135.1 0.7 copy-start.9
  352.7 7.1 %copy-start.3 = (f32[384,512]{0,1:T(8,128)S(1)}, f32[384,512]{0,1:T(8,128)}, u32[]{:S(2)}) copy-start(f32[384,512]{0,1:T(8,128)} %reduce-scatter.5.cloned.1.call-done) | copy-start | bytes 2359300
  354.4 8.1 %copy-start.8 = (f32[384,512]{0,1:T(8,128)S(1)}, f32[384,512]{0,1:T(8,128)}, u32[]{:S(2)}) copy-start(f32[384,512]{0,1:T(8,128)} %reduce-scatter.3.cloned.1.call-done) | copy-start | bytes 2359300
  356.1 141.1 %copy-start.4 = (f32[256,256]{1,0:T(8,128)S(1)}, f32[256,256]{1,0:T(8,128)}, u32[]{:S(2)}) copy-start(f32[256,256]{1,0:T(8,128)} %param.12) | copy-start | bytes 786436
  356.1 12.4 %all-to-all-start = ((f32[4,2,64,256]{3,2,1,0:T(8,128)}), f32[4,2,64,256]{3,2,1,0:T(8,128)S(1)}, u32[]{:S(2)}, u32[]{:S(2)}) async-start(f32[4,2,64,256]{3,2,1,0:T(8,128)} %copy.42), calls=%async_computation.2 | async-start | bytes 1048576 | tf_op jit(solution)/shard_map/all_to_all | solution.py:42
  359.8 137.5 %all-reduce.3.cloned.1.call-start = ((), (), s32[]{:S(2)}) async-start(), calls=%async_computation.7 | async-start | bytes 1572864 | tf_op jit(solution)/shard_map/psum | solution.py:102
  361.1 139.2 %copy-start.5 = (f32[256,256]{1,0:T(8,128)S(1)}, f32[256,256]{1,0:T(8,128)}, u32[]{:S(2)}) copy-start(f32[256,256]{1,0:T(8,128)} %param.16) | copy-start | bytes 786436
  498.8 5.2 %copy-start.6 = (f32[256,256]{1,0:T(8,128)}, f32[256,256]{1,0:T(8,128)S(1)}, u32[]{:S(2)}) copy-start(f32[256,256]{1,0:T(8,128)S(1)} %convolution_subtract_fusion.1) | copy-start | bytes 786436
  500.3 3.8 copy-start.7
Sparse Core Ops, SparseCore 0:
  50.1 22.3 all-gather.2
  87.2 22.3 all-gather.4
  113.2 118.7 reduce-scatter.2
  235.4 117.2 reduce-scatter.4
  366.3 130.8 all-reduce.2
where the time goes:
time: 511 us
  waiting for transfers between devices  348 us (68%)
  local copies, waits for them, and re-layouts  82.7 us (16%)
  matrix products  50.7 us (10%)
  between operations  14.1 us (3%)
  other arithmetic  10.7 us (2%)
    psum x1, waiting for transfers between devices, local(): lax.psum((partial_gram, partial_cross), ('row', 'col'))  129 us
    reduce_scatter x1, waiting for transfers between devices, local(): lax.psum_scatter(product_term(ancestor_inverse, gathered_two, place(gathe...  120 us
    reduce_scatter x1, waiting for transfers between devices, local(): lax.psum_scatter(product_term(ancestor_inverse, gathered_one, place(gathe...  96 us
    dot_general x5, matrix products, contract_rows(): lax.dot_general(left, right, (((0,), (0,)), ((), ())), precision=lax.Prec...  42.4 us
    scatter x1, local copies, waits for them, and re-layouts, local(): mask_one = jnp.zeros((ANC,), jnp.float32).at[struct_one].set(1.0)  39.8 us
    scatter x1, local copies, waits for them, and re-layouts, local(): mask_two = jnp.zeros((ANC,), jnp.float32).at[struct_two].set(1.0)  34.2 us
  transfers between devices with their start and end apart: 6, of which 4 were waited for; matrix products, arithmetic and copies ran while one was open for 17% of the time, Pallas kernels for 0%

commit v1 on v0

--- a/solution.py
+++ b/solution.py
@@ -99,7 +99,7 @@
     inverse_one = -product_one * result_mask_one
     partial_gram = contract_rows(resident_one, inverse_one)
     partial_cross = contract_rows(inverse_one, resident_two)
-    gram_one, cross_sum = lax.psum((partial_gram, partial_cross), ("row", "col"))
+    gram_one, cross_sum = lax.psum(lax.psum((partial_gram, partial_cross), "col"), "row")
     diag_one = matmul(lower_one.T, lower_one) - gram_one
     cross_two = -(cross_sum + matmul(diag_one, panel_above))
     inverse_two = -(product_two + matmul(inverse_one, panel_above)) * result_mask_two

time: 511 us -> 609 us (1.19)
  waiting for transfers between devices: 348 us -> 444 us
    psum x1 -> x3, waiting for transfers between devices: 129 us -> 230 us  [the longest x1 127 us: local(): gram_two = lax.psum(partial_second, ('row', 'col'))]
  transfers between devices with their start and end apart: 6 -> 8, of which waited for: 4 -> 5; matrix products, arithmetic and copies ran while one was open for 17% -> 15% of each run, Pallas kernels for 0% -> 0%
where the time goes in v1:
time: 609 us; the launch traced here: 608 us
  waiting for transfers between devices  444 us (73%)
  local copies, waits for them, and re-layouts  82.7 us (14%)
  matrix products  52.6 us (9%)
  between operations  14.4 us (2%)
  other arithmetic  10.7 us (2%)
    psum x1, waiting for transfers between devices, local(): gram_two = lax.psum(partial_second, ('row', 'col'))  127 us
    reduce_scatter x1, waiting for transfers between devices, local(): lax.psum_scatter(product_term(ancestor_inverse, gathered_two, place(gathe...  117 us
    reduce_scatter x1, waiting for transfers between devices, local(): lax.psum_scatter(product_term(ancestor_inverse, gathered_one, place(gathe...  96 us
    psum x1, waiting for transfers between devices, local(): lax.psum(lax.psum((partial_gram, partial_cross), 'col'), 'row')  73.7 us
    dot_general x5, matrix products, contract_rows(): lax.dot_general(left, right, (((0,), (0,)), ((), ())), precision=lax.Prec...  44.5 us
    scatter x1, local copies, waits for them, and re-layouts, local(): mask_one = jnp.zeros((ANC,), jnp.float32).at[struct_one].set(1.0)  39.8 us
    scatter x1, local copies, waits for them, and re-layouts, local(): mask_two = jnp.zeros((ANC,), jnp.float32).at[struct_two].set(1.0)  34.2 us
    psum x1, waiting for transfers between devices, local(): lax.psum((partial_gram, partial_cross), 'col')  29.9 us
  transfers between devices with their start and end apart: 8, of which 5 were waited for; matrix products, arithmetic and copies ran while one was open for 15% of the time, Pallas kernels for 0%

profile of v1, /device:TPU:0, one launch (start us, length us, event | category | flops | bytes accessed | tf_op | source)
XLA Modules:
  0.0 608.2 jit_solution(10648747044272336960)
XLA Ops:
  7.2 0.8 compare_select_fusion
  8.1 1.2 copy.36
  9.2 39.8 %scatter_custom_fusion = f32[12288]{0:T(1024)S(1)} fusion(s32[10752]{0:T(1024)S(1)} %compare_select_fusion, f32[10752]{0:T(1024)S(1)} %broadcast.48, f32[]{:T(128)} %constant.23.clone.1), kind=kCustom, calls=%fused_computation.34 | custom fusion | bytes 49156 | tf_op jit(solution)/shard_map/scatter | solution.py:66
  49.2 0.8 broadcast_multiply_fusion.1
  50.0 1.2 copy.37
  51.2 0.8 compare_select_fusion.1
  52.0 34.2 %scatter_custom_fusion.1 = f32[12288]{0:T(1024)S(1)} fusion(s32[9216]{0:T(1024)S(1)} %compare_select_fusion.1, f32[9216]{0:T(1024)S(1)} %broadcast.49, f32[]{:T(128)} %constant.23.clone.1), kind=kCustom, calls=%fused_computation.32 | custom fusion | bytes 49156 | tf_op jit(solution)/shard_map/scatter | solution.py:67
  86.3 0.8 broadcast_multiply_fusion
  87.5 1.0 copy-done.1
  88.7 19.2 %convolution_bitcast_fusion.1 = f32[3072,256]{0,1:T(8,128)S(1)} fusion(f32[1536,256]{0,1:T(8,128)S(1)} %copy-done.1, f32[1536,3072]{1,0:T(8,128)} %param.9), kind=kOutput, calls=%fused_computation.5 | convolution fusion | flops 14495514624 | bytes 23592960 | tf_op jit(solution)/shard_map/dot_general | solution.py:15
  107.9 3.1 pad_maximum_fusion
  111.6 1.0 copy-done.2
  112.8 19.2 %convolution_bitcast_fusion = f32[3072,256]{0,1:T(8,128)S(1)} fusion(f32[1536,256]{0,1:T(8,128)S(1)} %copy-done.2, f32[1536,3072]{1,0:T(8,128)} %param.9), kind=kOutput, calls=%fused_computation.4 | convolution fusion | flops 14495514624 | bytes 23592960 | tf_op jit(solution)/shard_map/dot_general | solution.py:15
  132.0 3.0 pad_maximum_fusion.1
  136.0 96.0 %reduce-scatter.3.cloned.1.call-done = f32[384,512]{0,1:T(8,128)} async-done(((f32[3072,512]{0,1:T(8,128)}), f32[384,512]{0,1:T(8,128)}) %reduce-scatter.3.cloned.1.call-update) | async-done | bytes 786448 | tf_op jit(solution)/shard_map/reduce_scatter | solution.py:82
  231.9 1.0 fusion.9
  233.0 2.3 fusion.7
  235.3 117.4 %reduce-scatter.5.cloned.1.call-done = f32[384,512]{0,1:T(8,128)} async-done(((f32[3072,512]{0,1:T(8,128)}), f32[384,512]{0,1:T(8,128)}) %reduce-scatter.5.cloned.1.call-update) | async-done | bytes 786448 | tf_op jit(solution)/shard_map/reduce_scatter | solution.py:89
  352.7 2.4 fusion.12
  355.2 1.6 fusion.1
  356.8 1.3 fusion.10
  358.4 29.9 %all-reduce.10.cloned.1.call-done = (f32[256,256]{1,0:T(8,128)}, f32[256,256]{1,0:T(8,128)}) async-done(((f32[256,256]{1,0:T(8,128)}, f32[256,256]{1,0:T(8,128)}), (f32[256,256]{1,0:T(8,128)}, f32[256,256]{1,0:T(8,128)})) %all-reduce.10.cloned.1.call-update) | async-done | bytes 524304 | tf_op jit(solution)/shard_map/psum | solution.py:102
  389.0 0.9 copy.42
  389.9 3.5 all-to-all-start
  393.4 0.9 copy.43
  394.3 126.6 %all-reduce.6.cloned.1.call-done = f32[256,256]{1,0:T(8,128)} async-done(((f32[256,256]{1,0:T(8,128)}), f32[256,256]{1,0:T(8,128)}) %all-reduce.6.cloned.1.call-update) | async-done | bytes 262160 | tf_op jit(solution)/shard_map/psum | solution.py:107
  520.9 1.5 convolution_subtract_fusion
  522.5 73.7 %all-reduce.8.cloned.1.call-done = (f32[256,256]{1,0:T(8,128)}, f32[256,256]{1,0:T(8,128)}) async-done(((f32[256,256]{1,0:T(8,128)}, f32[256,256]{1,0:T(8,128)}), (f32[256,256]{1,0:T(8,128)}, f32[256,256]{1,0:T(8,128)})) %all-reduce.8.cloned.1.call-update) | async-done | bytes 524304 | tf_op jit(solution)/shard_map/psum | solution.py:102
  596.2 1.5 convolution_subtract_fusion.1
  597.8 1.4 fusion.3
  599.2 1.3 fusion.2
  600.5 0.8 copy.61
  (48 shorter events, 3.4 us)
Async XLA Ops:
  7.2 348.0 %copy-start = (f32[256,256]{1,0:T(8,128)S(1)}, f32[256,256]{1,0:T(8,128)}, u32[]{:S(2)}) copy-start(f32[256,256]{1,0:T(8,128)} %param.15) | copy-start | bytes 786436
  7.2 80.0 %all-gather.3.cloned.1.call-start = ((), (), s32[]{:S(2)}) async-start(), calls=%async_computation.3 | async-start | bytes 1966080 | tf_op jit(solution)/shard_map/all_gather | solution.py:81
  50.0 61.3 %all-gather.5.cloned.1.call-start = ((), (), s32[]{:S(2)}) async-start(), calls=%async_computation.5 | async-start | bytes 1966080 | tf_op jit(solution)/shard_map/all_gather | solution.py:88
  87.1 144.9 %reduce-scatter.3.cloned.1.call-start = ((), (), s32[]{:S(2)}) async-start(), calls=%async_computation.4 | async-start | bytes 7077888 | tf_op jit(solution)/shard_map/reduce_scatter | solution.py:82
  87.2 1.4 copy-start.1
  111.0 241.7 %reduce-scatter.5.cloned.1.call-start = ((), (), s32[]{:S(2)}) async-start(), calls=%async_computation.6 | async-start | bytes 7077888 | tf_op jit(solution)/shard_map/reduce_scatter | solution.py:89
  111.3 1.4 copy-start.2
  135.1 0.7 copy-start.8
  135.1 253.2 %all-reduce.10.cloned.1.call-start = ((), (), s32[]{:S(2)}) async-start(), calls=%async_computation.9 | async-start | bytes 1048576 | tf_op jit(solution)/shard_map/psum | solution.py:102
  352.7 4.1 copy-start.3
  355.1 165.8 %all-reduce.6.cloned.1.call-start = ((), (), s32[]{:S(2)}) async-start(), calls=%async_computation.7 | async-start | bytes 524288 | tf_op jit(solution)/shard_map/psum | solution.py:107
  356.8 164.1 %copy-start.4 = (f32[256,256]{1,0:T(8,128)S(1)}, f32[256,256]{1,0:T(8,128)}, u32[]{:S(2)}) copy-start(f32[256,256]{1,0:T(8,128)} %param.16) | copy-start | bytes 786436
  358.2 238.1 %all-reduce.8.cloned.1.call-start = ((), (), s32[]{:S(2)}) async-start(), calls=%async_computation.8 | async-start | bytes 1048576 | tf_op jit(solution)/shard_map/psum | solution.py:102
  358.2 238.0 %copy-start.5 = (f32[256,256]{1,0:T(8,128)S(1)}, f32[256,256]{1,0:T(8,128)}, u32[]{:S(2)}) copy-start(f32[256,256]{1,0:T(8,128)} %param.12) | copy-start | bytes 786436
  389.9 132.6 %all-to-all-start = ((f32[4,2,64,256]{3,2,1,0:T(8,128)}), f32[4,2,64,256]{3,2,1,0:T(8,128)S(1)}, u32[]{:S(2)}, u32[]{:S(2)}) async-start(f32[4,2,64,256]{3,2,1,0:T(8,128)} %copy.42), calls=%async_computation.2 | async-start | bytes 1048576 | tf_op jit(solution)/shard_map/all_to_all | solution.py:42
  597.8 3.6 copy-start.6
  599.2 2.1 copy-start.7
Sparse Core Ops, SparseCore 0:
  50.1 22.3 all-gather.2
  87.2 22.3 all-gather.4
  113.2 118.7 reduce-scatter.2
  235.4 117.2 reduce-scatter.4
  355.5 32.7 all-reduce.9
  394.2 126.6 all-reduce.5
  524.4 71.7 all-reduce.7
